TPU v7x, 256 devices: a whole 4x4x8 slice. The times are simulated.
256 devices in a mesh: orb: 8 (over z), ri: 8 (over y, core), pair: 4 (over x).
Axes of the slice: x: 4, y: 4, z: 8, core: 2. Of those that a mesh axis runs over, the one named last changes fastest.
Arguments:
- three_center: bfloat16 [4096, 64, 1024], P(('orb', 'ri', 'pair')), may hold values from -0.59765625 to 0.59765625
- block_dest: int32 [4096, 1], P('orb'), may hold values from 0 to 31; in each aligned block of 16 rows (0 to 15, 16 to 31, ...) at most 2 rows name the same one
- block_row: int32 [4096], P('orb'), may hold values from 0 to 7
- block_col: int32 [4096], P('orb'), may hold values from 0 to 7
- occ_density: bfloat16 [256, 256], P('orb'), may hold values from -0.375 to 0.375
- virt_density: bfloat16 [256, 256], P('orb'), may hold values from -0.375 to 0.375
- occ_mask: int32 [8, 8], P('orb'), may hold values 0 or 1
- virt_mask: int32 [8, 8], P('orb'), may hold values 0 or 1
Outputs:
- chi_slabs: float32 [16384, 64], P(('orb', 'ri', 'pair'))
Inputs may be any that keep to these rules, and one draw needn't show every extreme that they name: `block_dest`: in the 16 rows of one device, no owner is named by more than 2 rows.
All inputs are finite; a program needn't handle non-finite values. No bound on the sum of `occ_mask` or of `virt_mask` on one device may be relied on, other than what follows from the above.
Results may differ from a plain program's by a relative error of at most 0.0047.
Values may be sent and summed in bfloat16 or wider, within the bound.
No kernel may reach another device: no remote copies, remote signals or barrier semaphores. Data moves between devices by JAX's collectives and lax.ppermute only.
A program may use at most 192 MiB of HBM per device.

v0:
```python
import functools

import jax
import jax.numpy as jnp
from jax import lax
from jax.experimental import pallas as pl
from jax.experimental.pallas import tpu as pltpu
from jax.sharding import PartitionSpec as P

BR = 64
BA = 32
CAP = 2
LANES = 128
PITCH = BR + 1
OWNER_BITS = 5
RELAY_SPAN_BITS = 6
RELAY_SPAN = 1 << RELAY_SPAN_BITS
RELAY_MASKS = (4, 1, 3, 8, 24)
RELAY_CAPS = (12, 2, 2, 2, 2)
NEAR_SHIFT = 4
NEAR_LOW = 0x0F0F0F0F
PLACE_BITS = 7
GROUP_BITS = 2
SCOPED = 12 * 1024 * 1024


def expand(mask_blocks, block_width):
    return jnp.repeat(jnp.repeat(mask_blocks, block_width, axis=0), block_width, axis=1)


def relay_offsets():
    offsets, total = [], 0
    for cap in RELAY_CAPS:
        offsets.append(total)
        total += cap
    return offsets, total


def groups_of(ao_blocks):
    return ao_blocks * ao_blocks >> GROUP_BITS


def bit_of(word, index):
    return lax.shift_right_logical(word, index) & 1


def pack_kernel(
    owners, blocks_dev, me_ref, dest_ref, blocks_ref, out_ref, late_ref, route_ref,
    named_ref, direct_ref, second_ref, used_ref, place_ref, rank_ref, kept_ref, sem,
):
    me = me_ref[0]
    offsets, relays = relay_offsets()

    def tally(s):
        bits = [lax.shift_left(jnp.int32(1), dest_ref[s * blocks_dev + k]) for k in range(blocks_dev)]
        named = functools.reduce(lax.bitwise_or, bits)
        return named, functools.reduce(lax.add, bits) - named

    def clear(o, _):
        rank_ref[o] = 0
        return 0

    lax.fori_loop(0, owners, clear, 0)
    twice = tally(me)[1]
    low = jnp.int32(NEAR_LOW)
    near_twice = lax.shift_left(twice & low, NEAR_SHIFT) | (lax.shift_right_logical(twice, NEAR_SHIFT) & low)

    def send_early(k, _):
        owner = dest_ref[me * blocks_dev + k]
        rank = rank_ref[owner]
        rank_ref[owner] = rank + 1
        early = (rank == 0) & (bit_of(near_twice, owner) == 0)
        kept_ref[k] = jnp.where(early, -1, rank)

        @pl.when(early)
        def _():
            pltpu.make_async_copy(blocks_ref.at[k], out_ref.at[owner], sem).start()

        return 0

    lax.fori_loop(0, blocks_dev, send_early, 0)

    def list_seconds(s, total):
        seen = jnp.int32(0)
        for k in range(blocks_dev):
            owner = dest_ref[s * blocks_dev + k]
            second_ref[total] = s * owners + owner
            total = total + bit_of(seen, owner)
            seen = seen | lax.shift_left(jnp.int32(1), owner)
        return total

    def start(s, total):
        named, doubled = tally(s)
        total = lax.cond(doubled != 0, lambda: list_seconds(s, total), lambda: total)
        named_ref[s] = named
        direct_ref[s] = named
        route_ref[s] = s
        route_ref[owners + s] = owners + relays + s
        place_ref[s] = s
        for m in range(len(RELAY_MASKS)):
            used_ref[m * owners + s] = 0
        return total

    seconds = lax.fori_loop(0, owners, start, jnp.int32(0))
    head = 2 * owners
    route_ref[head + 1] = 0

    def record(s, via, owner, rank, mask_index, place):
        @pl.when(owner == me)
        def _():
            route_ref[rank * owners + s] = owners + place

        @pl.when(via == me)
        def _():
            count = route_ref[head + 1]
            route_ref[head + 2 + count] = s * RELAY_SPAN + place
            route_ref[head + 1] = count + 1

        @pl.when(s == me)
        def _():
            place_ref[rank * owners + owner] = via

    def room(mask_index, owner):
        return used_ref[mask_index * owners + owner] < RELAY_CAPS[mask_index]

    def route(e, failed):
        pair = second_ref[e]
        s, owner = lax.shift_right_logical(pair, OWNER_BITS), pair & (owners - 1)
        named = named_ref[s]
        near = owner ^ RELAY_MASKS[0]
        core_room = room(0, owner)
        choices = [(bit_of(named, near) == 0) & core_room]
        for m in range(1, len(RELAY_MASKS)):
            choices.append((bit_of(named, owner ^ RELAY_MASKS[m]) == 0) & room(m, owner))
        swap = core_room & (bit_of(direct_ref[s], near) == 1)
        for m in range(1, len(RELAY_MASKS)):
            choices.append(swap & (bit_of(named, near ^ RELAY_MASKS[m]) == 0) & room(m, near))
        choice = jnp.int32(len(choices))
        for c in reversed(range(len(choices))):
            choice = jnp.where(choices[c], jnp.int32(c), choice)
        for c in range(len(choices)):
            m = c if c < len(RELAY_MASKS) else c - len(RELAY_MASKS) + 1

            @pl.when(choice == c)
            def _():
                target = owner if c < len(RELAY_MASKS) else near
                via = target ^ RELAY_MASKS[m]
                count = used_ref[m * owners + target]
                used_ref[m * owners + target] = count + 1
                named_ref[s] = named | lax.shift_left(jnp.int32(1), via)
                record(s, via, target, 1 if c < len(RELAY_MASKS) else 0, m, offsets[m] + count)
                if c >= len(RELAY_MASKS):
                    direct_ref[s] = direct_ref[s] ^ lax.shift_left(jnp.int32(1), near)
                    count = used_ref[owner]
                    used_ref[owner] = count + 1
                    record(s, near, owner, 1, 0, offsets[0] + count)

        return failed | (choice == len(choices)).astype(jnp.int32)

    failed = lax.fori_loop(0, seconds, route, jnp.int32(0))
    route_ref[head] = failed

    @pl.when(failed == 1)
    def _():
        def undo(s, _):
            route_ref[s] = s
            route_ref[owners + s] = owners + relays + s
            place_ref[s] = s
            return 0

        lax.fori_loop(0, owners, undo, 0)
        route_ref[head + 1] = 0

    def send(k, _):
        rank = kept_ref[k]

        @pl.when(rank >= 0)
        def _():
            owner = dest_ref[me * blocks_dev + k]
            late = (rank == 1) & (failed == 1)

            @pl.when(late)
            def _():
                pltpu.make_async_copy(blocks_ref.at[k], late_ref.at[owner], sem).start()

            @pl.when(jnp.logical_not(late))
            def _():
                slot = place_ref[rank * owners + owner]
                pltpu.make_async_copy(blocks_ref.at[k], out_ref.at[slot], sem).start()

        return 0

    lax.fori_loop(0, blocks_dev, send, 0)
    pltpu.make_async_copy(blocks_ref, out_ref.at[pl.ds(0, blocks_dev)], sem).wait()


def pack(me, dest, blocks, owners):
    blocks_dev = blocks.shape[0]
    smem = pl.BlockSpec(memory_space=pltpu.SMEM)
    hbm = pl.BlockSpec(memory_space=pl.ANY)
    slots = jax.ShapeDtypeStruct((owners,) + blocks.shape[1:], blocks.dtype)
    relays = relay_offsets()[1]
    return pl.pallas_call(
        functools.partial(pack_kernel, owners, blocks_dev),
        out_shape=(slots, slots, jax.ShapeDtypeStruct((2 * owners + 2 + relays,), jnp.int32)),
        in_specs=[smem, smem, pl.BlockSpec(memory_space=pltpu.VMEM)],
        out_specs=(hbm, hbm, smem),
        scratch_shapes=[
            pltpu.SMEM((owners,), jnp.int32),
            pltpu.SMEM((owners,), jnp.int32),
            pltpu.SMEM((owners * blocks_dev,), jnp.int32),
            pltpu.SMEM((len(RELAY_MASKS) * owners,), jnp.int32),
            pltpu.SMEM((2 * owners,), jnp.int32),
            pltpu.SMEM((owners,), jnp.int32),
            pltpu.SMEM((blocks_dev,), jnp.int32),
            pltpu.SemaphoreType.DMA,
        ],
        name="pack",
    )(me, dest, blocks)


def forward_kernel(owners, route_ref, recv_ref, *refs):
    relay_refs, stage_ref, sem = refs[: len(RELAY_MASKS)], refs[-2], refs[-1]
    offsets, relays = relay_offsets()
    head = 2 * owners
    count = route_ref[head + 1]

    def take(i, _):
        slot = lax.shift_right_logical(route_ref[head + 2 + i], RELAY_SPAN_BITS)
        pltpu.make_async_copy(recv_ref.at[slot], stage_ref.at[i], sem).start()
        return 0

    def give(i, _):
        place = route_ref[head + 2 + i] & (RELAY_SPAN - 1)
        for ref, offset, cap in zip(relay_refs, offsets, RELAY_CAPS):
            @pl.when((place >= offset) & (place < offset + cap))
            def _():
                pltpu.make_async_copy(stage_ref.at[i], ref.at[place - offset], sem).start()

        return 0

    def wait(i, _):
        pltpu.make_async_copy(recv_ref.at[0], stage_ref.at[0], sem).wait()
        return 0

    lax.fori_loop(0, count, take, 0)
    lax.fori_loop(0, count, wait, 0)
    lax.fori_loop(0, count, give, 0)
    lax.fori_loop(0, count, wait, 0)


def forward(route, recv):
    owners = recv.shape[0]
    hbm = pl.BlockSpec(memory_space=pl.ANY)
    block = recv.shape[1:]
    return pl.pallas_call(
        functools.partial(forward_kernel, owners),
        out_shape=tuple(jax.ShapeDtypeStruct((cap,) + block, recv.dtype) for cap in RELAY_CAPS),
        in_specs=[pl.BlockSpec(memory_space=pltpu.SMEM), hbm],
        out_specs=(hbm,) * len(RELAY_CAPS),
        scratch_shapes=[pltpu.VMEM((relay_offsets()[1],) + block, recv.dtype), pltpu.SemaphoreType.DMA],
        name="forward",
    )(route, recv)


def plan_kernel(
    owners, blocks_dev, ao_blocks, me_ref, dest_ref, row_ref, col_ref, route_ref, table_ref, mine_ref
):
    me = me_ref[0]
    most = owners * CAP
    cells = ao_blocks * ao_blocks

    def clear(c, _):
        table_ref[c] = most
        return 0

    lax.fori_loop(0, cells, clear, 0)
    tail = cells + 2 * most + 1
    for r in range(ao_blocks + groups_of(ao_blocks)):
        table_ref[tail + r] = 0

    def scan(s, total):
        for k in range(blocks_dev):
            index = s * blocks_dev + k
            mine_ref[total] = index
            total = total + (dest_ref[index] == me).astype(jnp.int32)
        return total

    count = lax.fori_loop(0, owners, scan, jnp.int32(0))
    table_ref[cells + 2 * most] = count

    def enter(i, before):
        index = mine_ref[i]
        s = lax.div(index, blocks_dev)
        row = row_ref[index]
        cell = row * ao_blocks + col_ref[index]
        table_ref[cells + i] = table_ref[cell]
        table_ref[cell] = i
        place = route_ref[jnp.where(s == before, owners, 0) + s]
        table_ref[cells + most + i] = place | lax.shift_left(row, PLACE_BITS)
        late = (place >= owners).astype(jnp.int32)
        table_ref[tail + row] += 1 - late
        table_ref[tail + ao_blocks + lax.shift_right_logical(cell, GROUP_BITS)] += late
        return s

    lax.fori_loop(0, count, enter, jnp.int32(-1))


def plan(me, dest, row, col, route, owners, blocks_dev, ao_blocks):
    smem = pl.BlockSpec(memory_space=pltpu.SMEM)
    most = owners * CAP
    return pl.pallas_call(
        functools.partial(plan_kernel, owners, blocks_dev, ao_blocks),
        out_shape=jax.ShapeDtypeStruct((ao_blocks * ao_blocks + 2 * most + 1 + ao_blocks + groups_of(ao_blocks),), jnp.int32),
        in_specs=[smem] * 5,
        out_specs=smem,
        scratch_shapes=[pltpu.SMEM((most + 1,), jnp.int32)],
        name="plan",
    )(me, dest, row, col, route)


def merge_cells(most, ao_blocks, first_cell, table_ref, held, total):
    cells = ao_blocks * ao_blocks

    def merge(c, _):
        first = table_ref[c]

        @pl.when(first < most)
        def _():
            second = table_ref[cells + first]

            @pl.when(second < most)
            def _():
                total[...] = held[first].astype(jnp.float32)

                def add(slot):
                    total[...] += held[slot].astype(jnp.float32)
                    return table_ref[cells + slot]

                lax.while_loop(lambda slot: slot < most, add, second)
                held[first] = total[...].astype(held.dtype)

        return 0

    lax.fori_loop(first_cell, first_cell + (1 << GROUP_BITS), merge, 0)


def pair_shuffle():
    lane, to = (lax.broadcasted_iota(jnp.int32, (2 * LANES, 2 * LANES), axis) for axis in (0, 1))
    target = ((lane & 32) << 2) | (lane & 64) | ((lane & 128) >> 2) | (lane & 31)
    return (to == target).astype(jnp.float32).astype(jnp.bfloat16)


def place_group(first_cell, r, tile, lanes, table_ref, shuffle, held, dense, work):
    high = BA // 4
    x = []
    for j in range(4):
        s = table_ref[first_cell + j]
        x.append(jnp.concatenate([held[s, :, hi * LANES : (hi + 1) * LANES] for hi in range(high)], axis=0))
    low = lax.broadcasted_iota(jnp.int32, x[0].shape, 1) < LANES // 2
    z = [None] * 4
    for a in (0, 1):
        z[a] = jnp.where(low, x[a], pltpu.roll(x[a + 2], LANES // 2, 1))
        z[a + 2] = jnp.where(low, pltpu.roll(x[a], LANES // 2, 1), x[a + 2])
    y = [
        jnp.dot(jnp.concatenate(z[a : a + 2], axis=1), shuffle, preferred_element_type=jnp.float32)
        for a in (0, 2)
    ]
    for hi in range(high):
        for j in range(4):
            mu = r * BA + hi * 4 + j
            part = y[j // 2][hi * BR : (hi + 1) * BR, (j % 2) * LANES : (j % 2 + 1) * LANES]
            work[tile, pl.ds(mu * PITCH, BR), :] = part
            dense[mu, :, lanes] = part.astype(jnp.bfloat16)


def assemble_kernel(most, ao_blocks, table_ref, recv_ref, held, dense, work, total, sem):
    cells = ao_blocks * ao_blocks
    per_tile = LANES // BA
    tiles = ao_blocks // per_tile
    tail = cells + 2 * most + 1

    def fetch(i, _):
        entry = table_ref[cells + most + i]
        place = entry & ((1 << PLACE_BITS) - 1)
        row = lax.shift_right_logical(entry, PLACE_BITS)

        @pl.when(place < recv_ref.shape[0])
        def _():
            pltpu.make_async_copy(recv_ref.at[place], held.at[i], sem.at[row]).start()

        return 0

    lax.fori_loop(0, table_ref[cells + 2 * most], fetch, 0)
    held[most] = jnp.zeros(held.shape[1:], held.dtype)
    shuffle = pair_shuffle()

    def row(r, _):
        def arrive(i, _):
            pltpu.make_async_copy(recv_ref.at[0], held.at[0], sem.at[r]).wait()
            return 0

        lax.fori_loop(0, table_ref[tail + r], arrive, 0)
        for tile in range(tiles):
            first_cell = r * ao_blocks + tile * per_tile

            @pl.when(table_ref[tail + ao_blocks + r * tiles + tile] == 0)
            def _():
                merge_cells(most, ao_blocks, first_cell, table_ref, held, total)
                lanes = slice(tile * LANES, (tile + 1) * LANES)
                place_group(first_cell, r, tile, lanes, table_ref, shuffle, held, dense, work)

        return 0

    lax.fori_loop(0, ao_blocks, row, 0)


def assemble(table, recv, most, ao_blocks):
    width = ao_blocks * BA
    vmem = pl.BlockSpec(memory_space=pltpu.VMEM)
    return pl.pallas_call(
        functools.partial(assemble_kernel, most, ao_blocks),
        out_shape=(
            pltpu.VMEM((most + 1, BR, BA * BA), jnp.bfloat16),
            pltpu.VMEM((width, BR, width), jnp.bfloat16),
            pltpu.VMEM((width // LANES, width * PITCH, LANES), jnp.float32),
        ),
        in_specs=[pl.BlockSpec(memory_space=pltpu.SMEM), pl.BlockSpec(memory_space=pl.ANY)],
        out_specs=(vmem, vmem, vmem),
        scratch_shapes=[pltpu.VMEM((BR, BA * BA), jnp.float32), pltpu.SemaphoreType.DMA((ao_blocks,))],
        compiler_params=pltpu.CompilerParams(vmem_limit_bytes=SCOPED),
        cost_estimate=pl.CostEstimate(flops=1 << 32, bytes_accessed=1 << 24, transcendentals=0),
        name="assemble",
    )(table, recv)


def slab_kernel(most, ao_blocks, table_ref, occ_ref, virt_ref, *refs):
    late_refs = refs[:-9]
    held, dense, work = refs[-6:-3]
    out_ref, total, sem = refs[-3:]
    width = ao_blocks * BA
    cells = ao_blocks * ao_blocks
    per_tile = LANES // BA
    tiles = width // LANES
    tail = cells + 2 * most + 1
    slots = most // CAP

    def fetch(i, late):
        place = table_ref[cells + most + i] & ((1 << PLACE_BITS) - 1)

        @pl.when(place >= slots)
        def _():
            offset = slots
            for ref in late_refs:
                @pl.when((place >= offset) & (place < offset + ref.shape[0]))
                def _():
                    pltpu.make_async_copy(ref.at[place - offset], held.at[i], sem).start()

                offset += ref.shape[0]

        return late + (place >= slots).astype(jnp.int32)

    late = lax.fori_loop(0, table_ref[cells + 2 * most], fetch, jnp.int32(0))

    def arrive(i, _):
        pltpu.make_async_copy(late_refs[0].at[0], held.at[0], sem).wait()
        return 0

    lax.fori_loop(0, late, arrive, 0)

    shuffle = pair_shuffle()

    def place(step, _):
        @pl.when(table_ref[tail + ao_blocks + step] > 0)
        def _():
            r, tile = step // tiles, step % tiles
            first_cell = step * per_tile
            merge_cells(most, ao_blocks, first_cell, table_ref, held, total)
            lanes = pl.ds(pl.multiple_of(tile * LANES, LANES), LANES)
            place_group(first_cell, r, tile, lanes, table_ref, shuffle, held, dense, work)

        return 0

    lax.fori_loop(0, groups_of(ao_blocks), place, 0)

    occ_t = occ_ref[...].astype(jnp.float32).T.astype(jnp.bfloat16)
    virt = virt_ref[...]

    def transform(i, _):
        for j in range(16):
            rows = pl.ds(i * 16 + j, width, stride=PITCH)
            part = jnp.concatenate([work[t, rows, :] for t in range(tiles)], axis=1).astype(jnp.bfloat16)
            half = jnp.dot(occ_t, part, preferred_element_type=jnp.float32).astype(jnp.bfloat16)
            both = jnp.dot(half, virt, preferred_element_type=jnp.float32)
            for t in range(tiles):
                work[t, rows, :] = both[:, t * LANES : (t + 1) * LANES]
        return 0

    lax.fori_loop(0, BR // 16, transform, 0)

    def contract(i, acc):
        left, right = [], []
        for j in range(32):
            mu = i * 32 + j
            left += [work[t, pl.ds(mu * PITCH, BR), :] for t in range(tiles)]
            right.append(dense[mu])
        return acc + lax.dot_general(
            jnp.concatenate(left, axis=1).astype(jnp.bfloat16),
            jnp.concatenate(right, axis=1),
            (((1,), (1,)), ((), ())),
            preferred_element_type=jnp.float32,
        )

    out_ref[...] = lax.fori_loop(0, width // 32, contract, jnp.zeros((BR, BR), jnp.float32))


def slab(table, occ, virt, late, assembled, most, ao_blocks):
    smem = pl.BlockSpec(memory_space=pltpu.SMEM)
    vmem = pl.BlockSpec(memory_space=pltpu.VMEM)
    first = 3 + len(late)
    return pl.pallas_call(
        functools.partial(slab_kernel, most, ao_blocks),
        out_shape=tuple(pltpu.VMEM(a.shape, a.dtype) for a in assembled)
        + (jax.ShapeDtypeStruct((BR, BR), jnp.float32),),
        in_specs=[smem, vmem, vmem] + [pl.BlockSpec(memory_space=pltpu.HBM)] * len(late) + [vmem] * 3,
        out_specs=(vmem,) * 4,
        input_output_aliases={first + i: i for i in range(3)},
        scratch_shapes=[pltpu.VMEM((BR, BA * BA), jnp.float32), pltpu.SemaphoreType.DMA],
        compiler_params=pltpu.CompilerParams(vmem_limit_bytes=SCOPED),
        name="slab",
    )(table, occ, virt, *late, *assembled)[3]


def body(
    three_center, block_dest, block_row, block_col, occ_density, virt_density, occ_mask, virt_mask
):
    owners = lax.axis_size(("ri", "pair"))
    blocks_dev = three_center.shape[0]
    ao_blocks = occ_mask.shape[1]
    width = occ_density.shape[1]
    me = lax.axis_index(("ri", "pair")).astype(jnp.int32).reshape(1)
    dest = block_dest.reshape(-1)
    outgoing, late, route = pack(me, dest, three_center, owners)
    group = ("ri", "pair")

    def exchange(slots):
        return lax.all_to_all(slots, group, split_axis=0, concat_axis=0, tiled=True)

    incoming = exchange(outgoing)
    local = jnp.concatenate(
        [
            occ_density * expand(occ_mask, BA).astype(jnp.bfloat16),
            virt_density * expand(virt_mask, BA).astype(jnp.bfloat16),
        ],
        axis=1,
    )
    need_late = jnp.broadcast_to(route[2 * owners].astype(jnp.bfloat16), (8, 2 * width))
    height = local.shape[0]
    gathered = lax.all_gather(jnp.concatenate([local, need_late], axis=0), "orb", axis=0, tiled=True)
    gathered = gathered.reshape(-1, height + 8, 2 * width)
    whole = gathered[:, :height].reshape(width, 2 * width)
    any_late = jnp.max(gathered[:, height, 0]) > 0
    table = plan(me, dest, block_row, block_col, route, owners, blocks_dev, ao_blocks)
    route, table, occ, virt, any_late = lax.optimization_barrier(
        (route, table, whole[:, :width], whole[:, width:], any_late)
    )
    incoming, late = lax.optimization_barrier((incoming, late))
    late = lax.cond(any_late, exchange, lambda slots: slots, late)
    relayed = [
        lax.ppermute(part, group, [(i, i ^ mask) for i in range(owners)])
        for part, mask in zip(forward(route, incoming), RELAY_MASKS)
    ]
    assembled = assemble(table, incoming, owners * CAP, ao_blocks)
    return slab(table, occ, virt, [*relayed, late], assembled, owners * CAP, ao_blocks)


def solution(mesh):
    placed = (
        P(("orb", "ri", "pair"), None, None),
        P("orb", None),
        P("orb"),
        P("orb"),
        P("orb", None),
        P("orb", None),
        P("orb", None),
        P("orb", None),
    )
    return jax.shard_map(
        body, mesh=mesh, in_specs=placed, out_specs=P(("orb", "ri", "pair"), None), check_vma=False
    )
```

profile of v0, /device:TPU:1, one launch (start us, length us, event | category | flops | bytes accessed | tf_op | source)
XLA Modules:
  0.0 93.5 jit_solution(4490717184802683747)
XLA Ops:
  0.0 5.4 %pack.1 = (bf16[32,64,1024]{2,1,0:T(8,128)(2,1)}, bf16[32,64,1024]{2,1,0:T(8,128)(2,1)}, s32[86]{0:T(128)}) custom-call(s32[1]{0:T(128)} %bitcast.me_ref, s32[512]{0:T(512)} %bitcast.12, bf16[16,64,1024]{2,1,0:T(8,128)(2,1)} %blocks_ref.1), custom_call_target="tpu_custom_call" | custom-call | tf_op jit(solution)/shard_map/pack/pallas_call | solution.py:203
  5.4 0.0 copy-start.6
  5.4 0.0 copy-start.7
  5.4 0.0 copy-start.5
  5.4 0.0 copy-start.3
  5.4 0.0 copy-start.4
  5.4 8.9 %all-to-all-start.1 = ((bf16[32,64,1024]{2,1,0:T(8,128)(2,1)}), bf16[32,64,1024]{2,1,0:T(8,128)(2,1)}, u32[]{:S(2)}, u32[]{:S(2)}) async-start(bf16[32,64,1024]{2,1,0:T(8,128)(2,1)} %get-tuple-element.34), calls=%async_computation.1 | async-start | bytes 8388608 | tf_op jit(solution)/shard_map/all_to_all | solution.py:547
  14.3 0.0 copy-done.6
  14.4 0.1 broadcast_in_dim.15
  14.4 0.1 convert_element_type.34
  14.5 0.0 copy-done.7
  14.5 0.1 broadcast_in_dim.13
  14.6 0.1 convert_element_type.31
  14.7 0.0 copy-done.5
  14.7 0.6 slice.16
  15.3 0.0 copy-done.3
  15.3 0.0 copy-done.4
  15.3 0.7 fusion.2
  16.0 24.9 %all_gather.3 = bf16[320,512]{1,0:T(8,128)(2,1)S(1)} all-gather(bf16[40,512]{1,0:T(8,128)(2,1)S(1)} %fusion.2), channel_id=1, replica_groups=mesh['orb'=8,'ri'=8,'pair'=4] {'orb'}, dimensions={0}, use_global_device_ids=true | all-gather | bytes 368640 | tf_op jit(solution)/shard_map/all_gather | solution.py:559
  40.9 3.9 %plan.1.table_ref = s32[217]{0:T(256)} custom-call(s32[1]{0:T(128)} %bitcast.me_ref, s32[512]{0:T(512)} %bitcast.13, s32[512]{0:T(512)} %row_ref.1, s32[512]{0:T(512)} %col_ref.1, s32[86]{0:T(128)} %get-tuple-element.33.route_ref), custom_call_target="tpu_custom_call" | custom-call | tf_op jit(solution)/shard_map/plan/pallas_call | solution.py:312
  44.8 0.6 slice_reduce_fusion
  46.0 17.9 %all-to-all-done.1.recv_ref = bf16[32,64,1024]{2,1,0:T(8,128)(2,1)} async-done(((bf16[32,64,1024]{2,1,0:T(8,128)(2,1)}), bf16[32,64,1024]{2,1,0:T(8,128)(2,1)}, u32[]{:S(2)}, u32[]{:S(2)}) %all-to-all-start.1) | async-done | bytes 4194336 | tf_op jit(solution)/shard_map/all_to_all | solution.py:547
  63.9 0.7 forward.1
  64.6 4.0 %collective-permute-start = (bf16[12,64,1024]{2,1,0:T(8,128)(2,1)}, bf16[12,64,1024]{2,1,0:T(8,128)(2,1)}, u32[]{:S(2)}, u32[]{:S(2)}) collective-permute-start(bf16[12,64,1024]{2,1,0:T(8,128)(2,1)} %get-tuple-element.37), channel_id=1, source_target_pairs={{0,4},{1,5},{2,6},{3,7},{4,0},{5,1},{6,2},{7,3},{8,12},{9,13},{10,... | collective-permute-start | bytes 4718600 | tf_op jit(solution)/shard_map/ppermute | solution.py:570
  68.6 1.2 %collective-permute-start.1 = (bf16[2,64,1024]{2,1,0:T(8,128)(2,1)}, bf16[2,64,1024]{2,1,0:T(8,128)(2,1)S(1)}, u32[]{:S(2)}, u32[]{:S(2)}) collective-permute-start(bf16[2,64,1024]{2,1,0:T(8,128)(2,1)} %get-tuple-element.38), channel_id=1, source_target_pairs={{0,1},{1,0},{2,3},{3,2},{4,5},{5,4},{6,7},{7,6},{8,9},{9,8},{10,11... | collective-permute-start | bytes 786440 | tf_op jit(solution)/shard_map/ppermute | solution.py:570
  69.8 0.0 collective-permute-start.2
  69.8 0.0 collective-permute-start.3
  69.8 0.0 copy-start
  69.8 0.6 collective-permute-start.4
  70.4 0.0 copy-done
  70.5 0.0 copy-start.1
  70.5 8.3 %assemble.1 = (bf16[65,64,1024]{2,1,0:T(8,128)(2,1)S(1)}, bf16[256,64,256]{2,1,0:T(8,128)(2,1)S(1)}, f32[2,16640,128]{2,1,0:T(8,128)S(1)}) custom-call(s32[217]{0:T(256)S(1)} %copy-done, bf16[32,64,1024]{2,1,0:T(8,128)(2,1)} %all-to-all-done.1.recv_ref), custom_call_target="tpu_custom_call" | custom-call | flops 4294967296 | bytes 16777216 | tf_op jit(solution)/shard_map/assemble/pallas_call | solution.py:421
  78.8 0.0 collective-permute-done.1.refs_1_
  78.8 0.0 collective-permute-done.2.refs_2_
  78.8 0.0 collective-permute-done.3.refs_3_
  78.8 0.0 collective-permute-done.4.refs_4_
  78.8 0.0 collective-permute-done.refs_0_
  78.8 0.0 copy-done.1
  78.8 14.6 %slab.1 = (bf16[65,64,1024]{2,1,0:T(8,128)(2,1)S(1)}, bf16[256,64,256]{2,1,0:T(8,128)(2,1)S(1)}, f32[2,16640,128]{2,1,0:T(8,128)S(1)}, f32[64,64]{1,0:T(8,128)}) custom-call(s32[217]{0:T(256)S(1)} %copy-done, bf16[256,256]{1,0:T(8,128)(2,1)S(1)} %get-tuple-element.31.occ_ref, ...), custom_call_target="tpu_custom_call", output_to_operand_aliasing={{0}: (9, {}), {1}: (10, {}), {2}: (11, {})} | custom-call | tf_op jit(solution)/shard_map/slab/pallas_call | solution.py:521
  (7 shorter events, 0.1 us)
Async XLA Ops:
  5.4 9.0 %copy-start.6 = (s32[1,8]{1,0:T(1,128)S(1)}, s32[1,8]{1,0:T(1,128)}, u32[]{:S(2)}) copy-start(s32[1,8]{1,0:T(1,128)} %param.17) | copy-start | bytes 100
  5.4 9.1 %copy-start.7 = (s32[1,8]{1,0:T(1,128)S(1)}, s32[1,8]{1,0:T(1,128)}, u32[]{:S(2)}) copy-start(s32[1,8]{1,0:T(1,128)} %param.16) | copy-start | bytes 100
  5.4 9.3 %copy-start.5 = (s32[86]{0:T(128)S(1)}, s32[86]{0:T(128)}, u32[]{:S(2)}) copy-start(s32[86]{0:T(128)} %get-tuple-element.33.route_ref) | copy-start | bytes 1036
  5.4 9.9 %copy-start.3 = (bf16[32,256]{1,0:T(8,128)(2,1)S(1)}, bf16[32,256]{1,0:T(8,128)(2,1)}, u32[]{:S(2)}) copy-start(bf16[32,256]{1,0:T(8,128)(2,1)} %param.15) | copy-start | bytes 49156
  5.4 9.9 %copy-start.4 = (bf16[32,256]{1,0:T(8,128)(2,1)S(1)}, bf16[32,256]{1,0:T(8,128)(2,1)}, u32[]{:S(2)}) copy-start(bf16[32,256]{1,0:T(8,128)(2,1)} %param.14) | copy-start | bytes 49156
  5.4 58.5 %all-to-all-start.1 = ((bf16[32,64,1024]{2,1,0:T(8,128)(2,1)}), bf16[32,64,1024]{2,1,0:T(8,128)(2,1)}, u32[]{:S(2)}, u32[]{:S(2)}) async-start(bf16[32,64,1024]{2,1,0:T(8,128)(2,1)} %get-tuple-element.34), calls=%async_computation.1 | async-start | bytes 8388608 | tf_op jit(solution)/shard_map/all_to_all | solution.py:547
  64.6 14.2 %collective-permute-start = (bf16[12,64,1024]{2,1,0:T(8,128)(2,1)}, bf16[12,64,1024]{2,1,0:T(8,128)(2,1)}, u32[]{:S(2)}, u32[]{:S(2)}) collective-permute-start(bf16[12,64,1024]{2,1,0:T(8,128)(2,1)} %get-tuple-element.37), channel_id=1, source_target_pairs={{0,4},{1,5},{2,6},{3,7},{4,0},{5,1},{6,2},{7,3},{8,12},{9,13},{10,... | collective-permute-start | bytes 4718600 | tf_op jit(solution)/shard_map/ppermute | solution.py:570
  68.6 10.2 %collective-permute-start.1 = (bf16[2,64,1024]{2,1,0:T(8,128)(2,1)}, bf16[2,64,1024]{2,1,0:T(8,128)(2,1)S(1)}, u32[]{:S(2)}, u32[]{:S(2)}) collective-permute-start(bf16[2,64,1024]{2,1,0:T(8,128)(2,1)} %get-tuple-element.38), channel_id=1, source_target_pairs={{0,1},{1,0},{2,3},{3,2},{4,5},{5,4},{6,7},{7,6},{8,9},{9,8},{10,11... | collective-permute-start | bytes 786440 | tf_op jit(solution)/shard_map/ppermute | solution.py:570
  69.8 9.0 %collective-permute-start.2 = (bf16[2,64,1024]{2,1,0:T(8,128)(2,1)}, bf16[2,64,1024]{2,1,0:T(8,128)(2,1)}, u32[]{:S(2)}, u32[]{:S(2)}) collective-permute-start(bf16[2,64,1024]{2,1,0:T(8,128)(2,1)} %get-tuple-element.39), channel_id=1, source_target_pairs={{0,3},{1,2},{2,1},{3,0},{4,7},{5,6},{6,5},{7,4},{8,11},{9,10},{10,... | collective-permute-start | bytes 786440 | tf_op jit(solution)/shard_map/ppermute | solution.py:570
  69.8 9.0 %collective-permute-start.3 = (bf16[2,64,1024]{2,1,0:T(8,128)(2,1)}, bf16[2,64,1024]{2,1,0:T(8,128)(2,1)}, u32[]{:S(2)}, u32[]{:S(2)}) collective-permute-start(bf16[2,64,1024]{2,1,0:T(8,128)(2,1)} %get-tuple-element.40), channel_id=1, source_target_pairs={{0,8},{1,9},{2,10},{3,11},{4,12},{5,13},{6,14},{7,15},{8,0},{9,1},... | collective-permute-start | bytes 786440 | tf_op jit(solution)/shard_map/ppermute | solution.py:570
  69.8 0.7 copy-start
  69.8 9.0 %collective-permute-start.4 = (bf16[2,64,1024]{2,1,0:T(8,128)(2,1)}, bf16[2,64,1024]{2,1,0:T(8,128)(2,1)}, u32[]{:S(2)}, u32[]{:S(2)}) collective-permute-start(bf16[2,64,1024]{2,1,0:T(8,128)(2,1)} %get-tuple-element.41), channel_id=1, source_target_pairs={{0,24},{1,25},{2,26},{3,27},{4,28},{5,29},{6,30},{7,31},{8,16},{9,... | collective-permute-start | bytes 786440 | tf_op jit(solution)/shard_map/ppermute | solution.py:570
  70.5 8.4 %copy-start.1 = (bf16[32,64,1024]{2,1,0:T(8,128)(2,1)S(1)}, bf16[32,64,1024]{2,1,0:T(8,128)(2,1)}, u32[]{:S(2)}) copy-start(bf16[32,64,1024]{2,1,0:T(8,128)(2,1)} %get-tuple-element.52.refs_5_) | copy-start | bytes 12582916
where the time goes:
time: 94.2 us; the launch traced here: 93.5 us
  Pallas kernels  32.9 us (35%)
  blocking collectives  24.9 us (26%)
  waiting for transfers between devices  17.9 us (19%)
  starting transfers between devices  14.7 us (16%)
  other arithmetic  1.29 us (1%)
  local copies, waits for them, and re-layouts  1.01 us (1%)
    all_gather x1, blocking collectives, body(): lax.all_gather(jnp.concatenate([local, need_late], axis=0), 'orb', axis=0...  24.9 us
    all_to_all x1, waiting for transfers between devices, exchange(): return lax.all_to_all(slots, group, split_axis=0, concat_axis=0, tiled=True)  17.9 us
    pallas_call x1, Pallas kernels, slab(): pl.pallas_call(functools.partial(slab_kernel, most, ao_blocks), out_shape...  14.6 us
    all_to_all x1, starting transfers between devices, exchange(): return lax.all_to_all(slots, group, split_axis=0, concat_axis=0, tiled=True)  8.91 us
    pallas_call x1, Pallas kernels, assemble(): pl.pallas_call(functools.partial(assemble_kernel, most, ao_blocks), out_s...  8.3 us
    ppermute x5, starting transfers between devices, body(): lax.ppermute(part, group, [(i, i ^ mask) for i in range(owners)])  5.82 us
    pallas_call x1, Pallas kernels, pack(): pl.pallas_call(functools.partial(pack_kernel, owners, blocks_dev), out_sh...  5.36 us
    pallas_call x1, Pallas kernels, plan(): pl.pallas_call(functools.partial(plan_kernel, owners, blocks_dev, ao_bloc...  3.88 us
  transfers between devices with their start and end apart: 6, of which 1 were waited for; matrix products, arithmetic and copies ran while one was open for 2% of the time, Pallas kernels for 13%

commit v1 on v0

--- a/solution.py
+++ b/solution.py
@@ -45,9 +45,11 @@
 
 
 def pack_kernel(
-    owners, blocks_dev, me_ref, dest_ref, blocks_ref, out_ref, late_ref, route_ref,
-    named_ref, direct_ref, second_ref, used_ref, place_ref, rank_ref, kept_ref, sem,
+    owners, blocks_dev, me_ref, dest_ref, source_ref, out_ref, late_ref, route_ref,
+    named_ref, direct_ref, second_ref, used_ref, place_ref, rank_ref, kept_ref, blocks_ref, load_sem, sem,
 ):
+    load = pltpu.make_async_copy(source_ref, blocks_ref, load_sem)
+    load.start()
     me = me_ref[0]
     offsets, relays = relay_offsets()
 
@@ -77,8 +79,6 @@
             pltpu.make_async_copy(blocks_ref.at[k], out_ref.at[owner], sem).start()
 
         return 0
-
-    lax.fori_loop(0, blocks_dev, send_early, 0)
 
     def list_seconds(s, total):
         seen = jnp.int32(0)
@@ -102,6 +102,8 @@
         return total
 
     seconds = lax.fori_loop(0, owners, start, jnp.int32(0))
+    load.wait()
+    lax.fori_loop(0, blocks_dev, send_early, 0)
     head = 2 * owners
     route_ref[head + 1] = 0
 
@@ -203,7 +205,7 @@
     return pl.pallas_call(
         functools.partial(pack_kernel, owners, blocks_dev),
         out_shape=(slots, slots, jax.ShapeDtypeStruct((2 * owners + 2 + relays,), jnp.int32)),
-        in_specs=[smem, smem, pl.BlockSpec(memory_space=pltpu.VMEM)],
+        in_specs=[smem, smem, hbm],
         out_specs=(hbm, hbm, smem),
         scratch_shapes=[
             pltpu.SMEM((owners,), jnp.int32),
@@ -213,6 +215,8 @@
             pltpu.SMEM((2 * owners,), jnp.int32),
             pltpu.SMEM((owners,), jnp.int32),
             pltpu.SMEM((blocks_dev,), jnp.int32),
+            pltpu.VMEM(blocks.shape, blocks.dtype),
+            pltpu.SemaphoreType.DMA,
             pltpu.SemaphoreType.DMA,
         ],
         name="pack",
@@ -220,18 +224,20 @@
 
 
 def forward_kernel(owners, route_ref, recv_ref, *refs):
-    relay_refs, stage_ref, sem = refs[: len(RELAY_MASKS)], refs[-2], refs[-1]
+    relay_refs = refs[: len(RELAY_MASKS)]
+    stage_ref, take_sem, sem = refs[-3:]
     offsets, relays = relay_offsets()
     head = 2 * owners
     count = route_ref[head + 1]
 
     def take(i, _):
         slot = lax.shift_right_logical(route_ref[head + 2 + i], RELAY_SPAN_BITS)
-        pltpu.make_async_copy(recv_ref.at[slot], stage_ref.at[i], sem).start()
+        pltpu.make_async_copy(recv_ref.at[slot], stage_ref.at[i], take_sem.at[i]).start()
         return 0
 
     def give(i, _):
         place = route_ref[head + 2 + i] & (RELAY_SPAN - 1)
+        pltpu.make_async_copy(recv_ref.at[0], stage_ref.at[i], take_sem.at[i]).wait()
         for ref, offset, cap in zip(relay_refs, offsets, RELAY_CAPS):
             @pl.when((place >= offset) & (place < offset + cap))
             def _():
@@ -240,11 +246,10 @@
         return 0
 
     def wait(i, _):
-        pltpu.make_async_copy(recv_ref.at[0], stage_ref.at[0], sem).wait()
+        pltpu.make_async_copy(stage_ref.at[0], relay_refs[0].at[0], sem).wait()
         return 0
 
     lax.fori_loop(0, count, take, 0)
-    lax.fori_loop(0, count, wait, 0)
     lax.fori_loop(0, count, give, 0)
     lax.fori_loop(0, count, wait, 0)
 
@@ -258,7 +263,11 @@
         out_shape=tuple(jax.ShapeDtypeStruct((cap,) + block, recv.dtype) for cap in RELAY_CAPS),
         in_specs=[pl.BlockSpec(memory_space=pltpu.SMEM), hbm],
         out_specs=(hbm,) * len(RELAY_CAPS),
-        scratch_shapes=[pltpu.VMEM((relay_offsets()[1],) + block, recv.dtype), pltpu.SemaphoreType.DMA],
+        scratch_shapes=[
+            pltpu.VMEM((relay_offsets()[1],) + block, recv.dtype),
+            pltpu.SemaphoreType.DMA((relay_offsets()[1],)),
+            pltpu.SemaphoreType.DMA,
+        ],
         name="forward",
     )(route, recv)
 
@@ -297,7 +306,7 @@
         table_ref[cells + i] = table_ref[cell]
         table_ref[cell] = i
         place = route_ref[jnp.where(s == before, owners, 0) + s]
-        table_ref[cells + most + i] = place | lax.shift_left(row, PLACE_BITS)
+        table_ref[cells + most + i] = place | lax.shift_left(lax.shift_right_logical(cell, GROUP_BITS), PLACE_BITS)
         late = (place >= owners).astype(jnp.int32)
         table_ref[tail + row] += 1 - late
         table_ref[tail + ao_blocks + lax.shift_right_logical(cell, GROUP_BITS)] += late
@@ -383,7 +392,7 @@
     def fetch(i, _):
         entry = table_ref[cells + most + i]
         place = entry & ((1 << PLACE_BITS) - 1)
-        row = lax.shift_right_logical(entry, PLACE_BITS)
+        row = lax.div(lax.shift_right_logical(entry, PLACE_BITS), tiles)
 
         @pl.when(place < recv_ref.shape[0])
         def _():
@@ -445,8 +454,10 @@
     tail = cells + 2 * most + 1
     slots = most // CAP
 
-    def fetch(i, late):
-        place = table_ref[cells + most + i] & ((1 << PLACE_BITS) - 1)
+    def fetch(i, _):
+        entry = table_ref[cells + most + i]
+        place = entry & ((1 << PLACE_BITS) - 1)
+        group = lax.shift_right_logical(entry, PLACE_BITS)
 
         @pl.when(place >= slots)
         def _():
@@ -454,25 +465,26 @@
             for ref in late_refs:
                 @pl.when((place >= offset) & (place < offset + ref.shape[0]))
                 def _():
-                    pltpu.make_async_copy(ref.at[place - offset], held.at[i], sem).start()
+                    pltpu.make_async_copy(ref.at[place - offset], held.at[i], sem.at[group]).start()
 
                 offset += ref.shape[0]
 
-        return late + (place >= slots).astype(jnp.int32)
-
-    late = lax.fori_loop(0, table_ref[cells + 2 * most], fetch, jnp.int32(0))
-
-    def arrive(i, _):
-        pltpu.make_async_copy(late_refs[0].at[0], held.at[0], sem).wait()
-        return 0
-
-    lax.fori_loop(0, late, arrive, 0)
-
+        return 0
+
+    lax.fori_loop(0, table_ref[cells + 2 * most], fetch, 0)
+    occ_t = occ_ref[...].astype(jnp.float32).T.astype(jnp.bfloat16)
     shuffle = pair_shuffle()
 
     def place(step, _):
-        @pl.when(table_ref[tail + ao_blocks + step] > 0)
-        def _():
+        late = table_ref[tail + ao_blocks + step]
+
+        @pl.when(late > 0)
+        def _():
+            def arrive(i, _):
+                pltpu.make_async_copy(late_refs[0].at[0], held.at[0], sem.at[step]).wait()
+                return 0
+
+            lax.fori_loop(0, late, arrive, 0)
             r, tile = step // tiles, step % tiles
             first_cell = step * per_tile
             merge_cells(most, ao_blocks, first_cell, table_ref, held, total)
@@ -483,7 +495,6 @@
 
     lax.fori_loop(0, groups_of(ao_blocks), place, 0)
 
-    occ_t = occ_ref[...].astype(jnp.float32).T.astype(jnp.bfloat16)
     virt = virt_ref[...]
 
     def transform(i, _):
@@ -525,7 +536,10 @@
         in_specs=[smem, vmem, vmem] + [pl.BlockSpec(memory_space=pltpu.HBM)] * len(late) + [vmem] * 3,
         out_specs=(vmem,) * 4,
         input_output_aliases={first + i: i for i in range(3)},
-        scratch_shapes=[pltpu.VMEM((BR, BA * BA), jnp.float32), pltpu.SemaphoreType.DMA],
+        scratch_shapes=[
+            pltpu.VMEM((BR, BA * BA), jnp.float32),
+            pltpu.SemaphoreType.DMA((groups_of(ao_blocks),)),
+        ],
         compiler_params=pltpu.CompilerParams(vmem_limit_bytes=SCOPED),
         name="slab",
     )(table, occ, virt, *late, *assembled)[3]

time: 94.2 us -> 93.4 us (level)
  the two profiles are of different devices: /device:TPU:1 before, /device:TPU:131 now
where the time goes in v1:
time: 93.4 us; the launch traced here: 93.8 us
  Pallas kernels  33.3 us (36%)
  waiting for transfers between devices  24.6 us (26%)
  blocking collectives  21.3 us (23%)
  starting transfers between devices  11.6 us (12%)
  other arithmetic  1.29 us (1%)
  local copies, waits for them, and re-layouts  0.99 us (1%)
    all_to_all x1, waiting for transfers between devices, exchange(): return lax.all_to_all(slots, group, split_axis=0, concat_axis=0, tiled=True)  23.3 us
    all_gather x1, blocking collectives, body(): lax.all_gather(jnp.concatenate([local, need_late], axis=0), 'orb', axis=0...  21.3 us
    pallas_call x1, Pallas kernels, slab(): pl.pallas_call(functools.partial(slab_kernel, most, ao_blocks), out_shape...  16.8 us
    all_to_all x1, starting transfers between devices, exchange(): return lax.all_to_all(slots, group, split_axis=0, concat_axis=0, tiled=True)  8.34 us
    pallas_call x1, Pallas kernels, assemble(): pl.pallas_call(functools.partial(assemble_kernel, most, ao_blocks), out_s...  5.82 us
    pallas_call x1, Pallas kernels, pack(): pl.pallas_call(functools.partial(pack_kernel, owners, blocks_dev), out_sh...  5.76 us
    pallas_call x1, Pallas kernels, plan(): pl.pallas_call(functools.partial(plan_kernel, owners, blocks_dev, ao_bloc...  4.04 us
    ppermute x5, starting transfers between devices, body(): lax.ppermute(part, group, [(i, i ^ mask) for i in range(owners)])  3.28 us
  transfers between devices with their start and end apart: 6, of which 3 were waited for; matrix products, arithmetic and copies ran while one was open for 2% of the time, Pallas kernels for 11%

profile of v1, /device:TPU:131, one launch (start us, length us, event | category | flops | bytes accessed | tf_op | source)
XLA Modules:
  0.0 93.8 jit_solution(6279642330460841060)
XLA Ops:
  0.0 5.8 %pack.1 = (bf16[32,64,1024]{2,1,0:T(8,128)(2,1)}, bf16[32,64,1024]{2,1,0:T(8,128)(2,1)}, s32[86]{0:T(128)}) custom-call(s32[1]{0:T(128)} %bitcast.me_ref, s32[512]{0:T(512)} %bitcast.12, bf16[16,64,1024]{2,1,0:T(8,128)(2,1)} %source_ref.1), custom_call_target="tpu_custom_call" | custom-call | tf_op jit(solution)/shard_map/pack/pallas_call | solution.py:205
  5.8 0.0 copy-start.6
  5.8 0.0 copy-start.7
  5.8 0.0 copy-start.5
  5.8 0.0 copy-start.3
  5.8 0.0 copy-start.4
  5.8 8.3 %all-to-all-start.1 = ((bf16[32,64,1024]{2,1,0:T(8,128)(2,1)}), bf16[32,64,1024]{2,1,0:T(8,128)(2,1)}, u32[]{:S(2)}, u32[]{:S(2)}) async-start(bf16[32,64,1024]{2,1,0:T(8,128)(2,1)} %get-tuple-element.34), calls=%async_computation.1 | async-start | bytes 8388608 | tf_op jit(solution)/shard_map/all_to_all | solution.py:561
  14.2 0.0 copy-done.6
  14.2 0.1 broadcast_in_dim.15
  14.3 0.1 convert_element_type.34
  14.4 0.0 copy-done.7
  14.4 0.1 broadcast_in_dim.13
  14.4 0.1 convert_element_type.31
  14.5 0.0 copy-done.5
  14.5 0.6 slice.16
  15.1 0.0 copy-done.3
  15.1 0.0 copy-done.4
  15.1 0.7 fusion.2
  15.8 21.3 %all_gather.3 = bf16[320,512]{1,0:T(8,128)(2,1)S(1)} all-gather(bf16[40,512]{1,0:T(8,128)(2,1)S(1)} %fusion.2), channel_id=1, replica_groups=mesh['orb'=8,'ri'=8,'pair'=4] {'orb'}, dimensions={0}, use_global_device_ids=true | all-gather | bytes 368640 | tf_op jit(solution)/shard_map/all_gather | solution.py:573
  37.2 4.0 %plan.1.table_ref = s32[217]{0:T(256)} custom-call(s32[1]{0:T(128)} %bitcast.me_ref, s32[512]{0:T(512)} %bitcast.13, s32[512]{0:T(512)} %row_ref.1, s32[512]{0:T(512)} %col_ref.1, s32[86]{0:T(128)} %get-tuple-element.33.route_ref), custom_call_target="tpu_custom_call" | custom-call | tf_op jit(solution)/shard_map/plan/pallas_call | solution.py:321
  41.2 0.6 slice_reduce_fusion
  42.4 23.3 %all-to-all-done.1.recv_ref = bf16[32,64,1024]{2,1,0:T(8,128)(2,1)} async-done(((bf16[32,64,1024]{2,1,0:T(8,128)(2,1)}), bf16[32,64,1024]{2,1,0:T(8,128)(2,1)}, u32[]{:S(2)}, u32[]{:S(2)}) %all-to-all-start.1) | async-done | bytes 4194336 | tf_op jit(solution)/shard_map/all_to_all | solution.py:561
  65.8 0.9 forward.1
  66.7 0.6 collective-permute-start
  67.2 0.0 collective-permute-start.1
  67.2 1.6 %collective-permute-start.2 = (bf16[2,64,1024]{2,1,0:T(8,128)(2,1)}, bf16[2,64,1024]{2,1,0:T(8,128)(2,1)}, u32[]{:S(2)}, u32[]{:S(2)}) collective-permute-start(bf16[2,64,1024]{2,1,0:T(8,128)(2,1)} %get-tuple-element.39), channel_id=1, source_target_pairs={{0,3},{1,2},{2,1},{3,0},{4,7},{5,6},{6,5},{7,4},{8,11},{9,10},{10,... | collective-permute-start | bytes 786440 | tf_op jit(solution)/shard_map/ppermute | solution.py:584
  68.8 0.1 collective-permute-start.3
  68.9 0.0 copy-start
  68.9 1.0 %collective-permute-start.4 = (bf16[2,64,1024]{2,1,0:T(8,128)(2,1)}, bf16[2,64,1024]{2,1,0:T(8,128)(2,1)}, u32[]{:S(2)}, u32[]{:S(2)}) collective-permute-start(bf16[2,64,1024]{2,1,0:T(8,128)(2,1)} %get-tuple-element.41), channel_id=1, source_target_pairs={{0,24},{1,25},{2,26},{3,27},{4,28},{5,29},{6,30},{7,31},{8,16},{9,... | collective-permute-start | bytes 786440 | tf_op jit(solution)/shard_map/ppermute | solution.py:584
  69.9 0.0 copy-done
  69.9 0.0 copy-start.1
  69.9 5.8 %assemble.1 = (bf16[65,64,1024]{2,1,0:T(8,128)(2,1)S(1)}, bf16[256,64,256]{2,1,0:T(8,128)(2,1)S(1)}, f32[2,16640,128]{2,1,0:T(8,128)S(1)}) custom-call(s32[217]{0:T(256)S(1)} %copy-done, bf16[32,64,1024]{2,1,0:T(8,128)(2,1)} %all-to-all-done.1.recv_ref), custom_call_target="tpu_custom_call" | custom-call | flops 4294967296 | bytes 16777216 | tf_op jit(solution)/shard_map/assemble/pallas_call | solution.py:430
  75.8 0.0 collective-permute-done.1.refs_1_
  75.8 0.0 collective-permute-done.2.refs_2_
  75.8 0.2 collective-permute-done.3.refs_3_
  75.9 1.0 %collective-permute-done.4.refs_4_ = bf16[2,64,1024]{2,1,0:T(8,128)(2,1)} collective-permute-done((bf16[2,64,1024]{2,1,0:T(8,128)(2,1)}, bf16[2,64,1024]{2,1,0:T(8,128)(2,1)}, u32[]{:S(2)}, u32[]{:S(2)}) %collective-permute-start.4) | collective-permute-done | bytes 262176 | tf_op jit(solution)/shard_map/ppermute | solution.py:584
  77.0 0.0 collective-permute-done.refs_0_
  77.0 0.0 copy-done.1
  77.0 16.8 %slab.1 = (bf16[65,64,1024]{2,1,0:T(8,128)(2,1)S(1)}, bf16[256,64,256]{2,1,0:T(8,128)(2,1)S(1)}, f32[2,16640,128]{2,1,0:T(8,128)S(1)}, f32[64,64]{1,0:T(8,128)}) custom-call(s32[217]{0:T(256)S(1)} %copy-done, bf16[256,256]{1,0:T(8,128)(2,1)S(1)} %get-tuple-element.31.occ_ref, ...), custom_call_target="tpu_custom_call", output_to_operand_aliasing={{0}: (9, {}), {1}: (10, {}), {2}: (11, {})} | custom-call | tf_op jit(solution)/shard_map/slab/pallas_call | solution.py:532
  (7 shorter events, 0.1 us)
Async XLA Ops:
  5.8 8.4 %copy-start.6 = (s32[1,8]{1,0:T(1,128)S(1)}, s32[1,8]{1,0:T(1,128)}, u32[]{:S(2)}) copy-start(s32[1,8]{1,0:T(1,128)} %param.17) | copy-start | bytes 100
  5.8 8.6 %copy-start.7 = (s32[1,8]{1,0:T(1,128)S(1)}, s32[1,8]{1,0:T(1,128)}, u32[]{:S(2)}) copy-start(s32[1,8]{1,0:T(1,128)} %param.16) | copy-start | bytes 100
  5.8 8.7 %copy-start.5 = (s32[86]{0:T(128)S(1)}, s32[86]{0:T(128)}, u32[]{:S(2)}) copy-start(s32[86]{0:T(128)} %get-tuple-element.33.route_ref) | copy-start | bytes 1036
  5.8 9.3 %copy-start.3 = (bf16[32,256]{1,0:T(8,128)(2,1)S(1)}, bf16[32,256]{1,0:T(8,128)(2,1)}, u32[]{:S(2)}) copy-start(bf16[32,256]{1,0:T(8,128)(2,1)} %param.15) | copy-start | bytes 49156
  5.8 9.3 %copy-start.4 = (bf16[32,256]{1,0:T(8,128)(2,1)S(1)}, bf16[32,256]{1,0:T(8,128)(2,1)}, u32[]{:S(2)}) copy-start(bf16[32,256]{1,0:T(8,128)(2,1)} %param.14) | copy-start | bytes 49156
  5.8 60.0 %all-to-all-start.1 = ((bf16[32,64,1024]{2,1,0:T(8,128)(2,1)}), bf16[32,64,1024]{2,1,0:T(8,128)(2,1)}, u32[]{:S(2)}, u32[]{:S(2)}) async-start(bf16[32,64,1024]{2,1,0:T(8,128)(2,1)} %get-tuple-element.34), calls=%async_computation.1 | async-start | bytes 8388608 | tf_op jit(solution)/shard_map/all_to_all | solution.py:561
  66.7 10.3 %collective-permute-start = (bf16[12,64,1024]{2,1,0:T(8,128)(2,1)}, bf16[12,64,1024]{2,1,0:T(8,128)(2,1)}, u32[]{:S(2)}, u32[]{:S(2)}) collective-permute-start(bf16[12,64,1024]{2,1,0:T(8,128)(2,1)} %get-tuple-element.37), channel_id=1, source_target_pairs={{0,4},{1,5},{2,6},{3,7},{4,0},{5,1},{6,2},{7,3},{8,12},{9,13},{10,... | collective-permute-start | bytes 4718600 | tf_op jit(solution)/shard_map/ppermute | solution.py:584
  67.2 8.5 %collective-permute-start.1 = (bf16[2,64,1024]{2,1,0:T(8,128)(2,1)}, bf16[2,64,1024]{2,1,0:T(8,128)(2,1)S(1)}, u32[]{:S(2)}, u32[]{:S(2)}) collective-permute-start(bf16[2,64,1024]{2,1,0:T(8,128)(2,1)} %get-tuple-element.38), channel_id=1, source_target_pairs={{0,1},{1,0},{2,3},{3,2},{4,5},{5,4},{6,7},{7,6},{8,9},{9,8},{10,11... | collective-permute-start | bytes 786440 | tf_op jit(solution)/shard_map/ppermute | solution.py:584
  67.2 8.6 %collective-permute-start.2 = (bf16[2,64,1024]{2,1,0:T(8,128)(2,1)}, bf16[2,64,1024]{2,1,0:T(8,128)(2,1)}, u32[]{:S(2)}, u32[]{:S(2)}) collective-permute-start(bf16[2,64,1024]{2,1,0:T(8,128)(2,1)} %get-tuple-element.39), channel_id=1, source_target_pairs={{0,3},{1,2},{2,1},{3,0},{4,7},{5,6},{6,5},{7,4},{8,11},{9,10},{10,... | collective-permute-start | bytes 786440 | tf_op jit(solution)/shard_map/ppermute | solution.py:584
  68.8 7.2 %collective-permute-start.3 = (bf16[2,64,1024]{2,1,0:T(8,128)(2,1)}, bf16[2,64,1024]{2,1,0:T(8,128)(2,1)}, u32[]{:S(2)}, u32[]{:S(2)}) collective-permute-start(bf16[2,64,1024]{2,1,0:T(8,128)(2,1)} %get-tuple-element.40), channel_id=1, source_target_pairs={{0,8},{1,9},{2,10},{3,11},{4,12},{5,13},{6,14},{7,15},{8,0},{9,1},... | collective-permute-start | bytes 786440 | tf_op jit(solution)/shard_map/ppermute | solution.py:584
  68.9 1.0 %copy-start = (s32[217]{0:T(256)S(1)}, s32[217]{0:T(256)}, u32[]{:S(2)}) copy-start(s32[217]{0:T(256)} %plan.1.table_ref) | copy-start | bytes 2608
  68.9 8.1 %collective-permute-start.4 = (bf16[2,64,1024]{2,1,0:T(8,128)(2,1)}, bf16[2,64,1024]{2,1,0:T(8,128)(2,1)}, u32[]{:S(2)}, u32[]{:S(2)}) collective-permute-start(bf16[2,64,1024]{2,1,0:T(8,128)(2,1)} %get-tuple-element.41), channel_id=1, source_target_pairs={{0,24},{1,25},{2,26},{3,27},{4,28},{5,29},{6,30},{7,31},{8,16},{9,... | collective-permute-start | bytes 786440 | tf_op jit(solution)/shard_map/ppermute | solution.py:584
  69.9 7.1 %copy-start.1 = (bf16[32,64,1024]{2,1,0:T(8,128)(2,1)S(1)}, bf16[32,64,1024]{2,1,0:T(8,128)(2,1)}, u32[]{:S(2)}) copy-start(bf16[32,64,1024]{2,1,0:T(8,128)(2,1)} %get-tuple-element.52.refs_5_) | copy-start | bytes 12582916

commit v2 on v1

--- a/solution.py
+++ b/solution.py
@@ -107,7 +107,7 @@
     head = 2 * owners
     route_ref[head + 1] = 0
 
-    def record(s, via, owner, rank, mask_index, place):
+    def record(s, via, owner, rank, place):
         @pl.when(owner == me)
         def _():
             route_ref[rank * owners + s] = owners + place
@@ -140,22 +140,28 @@
         choice = jnp.int32(len(choices))
         for c in reversed(range(len(choices))):
             choice = jnp.where(choices[c], jnp.int32(c), choice)
-        for c in range(len(choices)):
-            m = c if c < len(RELAY_MASKS) else c - len(RELAY_MASKS) + 1
-
-            @pl.when(choice == c)
+        swapped = choice >= len(RELAY_MASKS)
+        m = jnp.where(swapped, choice - len(RELAY_MASKS) + 1, choice)
+        mask, offset = jnp.int32(RELAY_MASKS[0]), jnp.int32(offsets[0])
+        for i in range(1, len(RELAY_MASKS)):
+            mask = jnp.where(m == i, RELAY_MASKS[i], mask)
+            offset = jnp.where(m == i, offsets[i], offset)
+        target = jnp.where(swapped, near, owner)
+        via = target ^ mask
+
+        @pl.when(choice < len(choices))
+        def _():
+            count = used_ref[m * owners + target]
+            used_ref[m * owners + target] = count + 1
+            named_ref[s] = named | lax.shift_left(jnp.int32(1), via)
+            record(s, via, target, jnp.where(swapped, 0, 1), offset + count)
+
+            @pl.when(swapped)
             def _():
-                target = owner if c < len(RELAY_MASKS) else near
-                via = target ^ RELAY_MASKS[m]
-                count = used_ref[m * owners + target]
-                used_ref[m * owners + target] = count + 1
-                named_ref[s] = named | lax.shift_left(jnp.int32(1), via)
-                record(s, via, target, 1 if c < len(RELAY_MASKS) else 0, m, offsets[m] + count)
-                if c >= len(RELAY_MASKS):
-                    direct_ref[s] = direct_ref[s] ^ lax.shift_left(jnp.int32(1), near)
-                    count = used_ref[owner]
-                    used_ref[owner] = count + 1
-                    record(s, near, owner, 1, 0, offsets[0] + count)
+                direct_ref[s] = direct_ref[s] ^ lax.shift_left(jnp.int32(1), near)
+                count = used_ref[owner]
+                used_ref[owner] = count + 1
+                record(s, near, owner, 1, offsets[0] + count)
 
         return failed | (choice == len(choices)).astype(jnp.int32)
 

time: 93.4 us -> 92.1 us (0.986)
  the two profiles are of different devices: /device:TPU:131 before, /device:TPU:120 now
where the time goes in v2:
time: 92.1 us; the launch traced here: 91.8 us
  Pallas kernels  32.6 us (35%)
  blocking collectives  25.5 us (28%)
  waiting for transfers between devices  17.8 us (19%)
  starting transfers between devices  12.8 us (14%)
  other arithmetic  1.29 us (1%)
  local copies, waits for them, and re-layouts  0.99 us (1%)
    all_gather x1, blocking collectives, body(): lax.all_gather(jnp.concatenate([local, need_late], axis=0), 'orb', axis=0...  25.5 us
    all_to_all x1, waiting for transfers between devices, exchange(): return lax.all_to_all(slots, group, split_axis=0, concat_axis=0, tiled=True)  17.4 us
    pallas_call x1, Pallas kernels, slab(): pl.pallas_call(functools.partial(slab_kernel, most, ao_blocks), out_shape...  15.4 us
    pallas_call x1, Pallas kernels, assemble(): pl.pallas_call(functools.partial(assemble_kernel, most, ao_blocks), out_s...  7.31 us
    all_to_all x1, starting transfers between devices, exchange(): return lax.all_to_all(slots, group, split_axis=0, concat_axis=0, tiled=True)  7.29 us
    ppermute x5, starting transfers between devices, body(): lax.ppermute(part, group, [(i, i ^ mask) for i in range(owners)])  5.5 us
    pallas_call x1, Pallas kernels, pack(): pl.pallas_call(functools.partial(pack_kernel, owners, blocks_dev), out_sh...  5.09 us
    pallas_call x1, Pallas kernels, plan(): pl.pallas_call(functools.partial(plan_kernel, owners, blocks_dev, ao_bloc...  3.97 us
  transfers between devices with their start and end apart: 6, of which 2 were waited for; matrix products, arithmetic and copies ran while one was open for 2% of the time, Pallas kernels for 12%

profile of v2, /device:TPU:120, one launch (start us, length us, event | category | flops | bytes accessed | tf_op | source)
XLA Modules:
  0.0 91.8 jit_solution(14821121030358180556)
XLA Ops:
  0.0 5.1 %pack.1 = (bf16[32,64,1024]{2,1,0:T(8,128)(2,1)}, bf16[32,64,1024]{2,1,0:T(8,128)(2,1)}, s32[86]{0:T(128)}) custom-call(s32[1]{0:T(128)} %bitcast.me_ref, s32[512]{0:T(512)} %bitcast.12, bf16[16,64,1024]{2,1,0:T(8,128)(2,1)} %source_ref.1), custom_call_target="tpu_custom_call" | custom-call | tf_op jit(solution)/shard_map/pack/pallas_call | solution.py:211
  5.1 0.0 copy-start.6
  5.1 0.0 copy-start.7
  5.1 0.0 copy-start.5
  5.1 0.0 copy-start.3
  5.1 0.0 copy-start.4
  5.2 7.3 %all-to-all-start.1 = ((bf16[32,64,1024]{2,1,0:T(8,128)(2,1)}), bf16[32,64,1024]{2,1,0:T(8,128)(2,1)}, u32[]{:S(2)}, u32[]{:S(2)}) async-start(bf16[32,64,1024]{2,1,0:T(8,128)(2,1)} %get-tuple-element.34), calls=%async_computation.1 | async-start | bytes 8388608 | tf_op jit(solution)/shard_map/all_to_all | solution.py:567
  12.5 0.0 copy-done.6
  12.5 0.1 broadcast_in_dim.15
  12.6 0.1 convert_element_type.34
  12.6 0.0 copy-done.7
  12.7 0.1 broadcast_in_dim.13
  12.7 0.1 convert_element_type.31
  12.8 0.0 copy-done.5
  12.8 0.6 slice.16
  13.4 0.0 copy-done.3
  13.4 0.0 copy-done.4
  13.4 0.7 fusion.2
  14.1 25.5 %all_gather.3 = bf16[320,512]{1,0:T(8,128)(2,1)S(1)} all-gather(bf16[40,512]{1,0:T(8,128)(2,1)S(1)} %fusion.2), channel_id=1, replica_groups=mesh['orb'=8,'ri'=8,'pair'=4] {'orb'}, dimensions={0}, use_global_device_ids=true | all-gather | bytes 368640 | tf_op jit(solution)/shard_map/all_gather | solution.py:579
  39.7 4.0 %plan.1.table_ref = s32[217]{0:T(256)} custom-call(s32[1]{0:T(128)} %bitcast.me_ref, s32[512]{0:T(512)} %bitcast.13, s32[512]{0:T(512)} %row_ref.1, s32[512]{0:T(512)} %col_ref.1, s32[86]{0:T(128)} %get-tuple-element.33.route_ref), custom_call_target="tpu_custom_call" | custom-call | tf_op jit(solution)/shard_map/plan/pallas_call | solution.py:327
  43.6 0.6 slice_reduce_fusion
  44.9 17.4 %all-to-all-done.1.recv_ref = bf16[32,64,1024]{2,1,0:T(8,128)(2,1)} async-done(((bf16[32,64,1024]{2,1,0:T(8,128)(2,1)}), bf16[32,64,1024]{2,1,0:T(8,128)(2,1)}, u32[]{:S(2)}, u32[]{:S(2)}) %all-to-all-start.1) | async-done | bytes 4194336 | tf_op jit(solution)/shard_map/all_to_all | solution.py:567
  62.3 0.9 forward.1
  63.1 1.7 %collective-permute-start = (bf16[12,64,1024]{2,1,0:T(8,128)(2,1)}, bf16[12,64,1024]{2,1,0:T(8,128)(2,1)}, u32[]{:S(2)}, u32[]{:S(2)}) collective-permute-start(bf16[12,64,1024]{2,1,0:T(8,128)(2,1)} %get-tuple-element.37), channel_id=1, source_target_pairs={{0,4},{1,5},{2,6},{3,7},{4,0},{5,1},{6,2},{7,3},{8,12},{9,13},{10,... | collective-permute-start | bytes 4718600 | tf_op jit(solution)/shard_map/ppermute | solution.py:590
  64.8 0.0 collective-permute-start.1
  64.8 1.8 %collective-permute-start.2 = (bf16[2,64,1024]{2,1,0:T(8,128)(2,1)}, bf16[2,64,1024]{2,1,0:T(8,128)(2,1)}, u32[]{:S(2)}, u32[]{:S(2)}) collective-permute-start(bf16[2,64,1024]{2,1,0:T(8,128)(2,1)} %get-tuple-element.39), channel_id=1, source_target_pairs={{0,3},{1,2},{2,1},{3,0},{4,7},{5,6},{6,5},{7,4},{8,11},{9,10},{10,... | collective-permute-start | bytes 786440 | tf_op jit(solution)/shard_map/ppermute | solution.py:590
  66.7 0.0 collective-permute-start.3
  66.7 0.0 copy-start
  66.7 2.0 %collective-permute-start.4 = (bf16[2,64,1024]{2,1,0:T(8,128)(2,1)}, bf16[2,64,1024]{2,1,0:T(8,128)(2,1)}, u32[]{:S(2)}, u32[]{:S(2)}) collective-permute-start(bf16[2,64,1024]{2,1,0:T(8,128)(2,1)} %get-tuple-element.41), channel_id=1, source_target_pairs={{0,24},{1,25},{2,26},{3,27},{4,28},{5,29},{6,30},{7,31},{8,16},{9,... | collective-permute-start | bytes 786440 | tf_op jit(solution)/shard_map/ppermute | solution.py:590
  68.7 0.0 copy-done
  68.7 0.0 copy-start.1
  68.7 7.3 %assemble.1 = (bf16[65,64,1024]{2,1,0:T(8,128)(2,1)S(1)}, bf16[256,64,256]{2,1,0:T(8,128)(2,1)S(1)}, f32[2,16640,128]{2,1,0:T(8,128)S(1)}) custom-call(s32[217]{0:T(256)S(1)} %copy-done, bf16[32,64,1024]{2,1,0:T(8,128)(2,1)} %all-to-all-done.1.recv_ref), custom_call_target="tpu_custom_call" | custom-call | flops 4294967296 | bytes 16777216 | tf_op jit(solution)/shard_map/assemble/pallas_call | solution.py:436
  76.0 0.0 collective-permute-done.1.refs_1_
  76.0 0.0 collective-permute-done.2.refs_2_
  76.0 0.0 collective-permute-done.3.refs_3_
  76.0 0.4 collective-permute-done.4.refs_4_
  76.4 0.0 collective-permute-done.refs_0_
  76.4 0.0 copy-done.1
  76.4 15.4 %slab.1 = (bf16[65,64,1024]{2,1,0:T(8,128)(2,1)S(1)}, bf16[256,64,256]{2,1,0:T(8,128)(2,1)S(1)}, f32[2,16640,128]{2,1,0:T(8,128)S(1)}, f32[64,64]{1,0:T(8,128)}) custom-call(s32[217]{0:T(256)S(1)} %copy-done, bf16[256,256]{1,0:T(8,128)(2,1)S(1)} %get-tuple-element.31.occ_ref, ...), custom_call_target="tpu_custom_call", output_to_operand_aliasing={{0}: (9, {}), {1}: (10, {}), {2}: (11, {})} | custom-call | tf_op jit(solution)/shard_map/slab/pallas_call | solution.py:538
  (7 shorter events, 0.1 us)
Async XLA Ops:
  5.1 7.4 %copy-start.6 = (s32[1,8]{1,0:T(1,128)S(1)}, s32[1,8]{1,0:T(1,128)}, u32[]{:S(2)}) copy-start(s32[1,8]{1,0:T(1,128)} %param.17) | copy-start | bytes 100
  5.1 7.5 %copy-start.7 = (s32[1,8]{1,0:T(1,128)S(1)}, s32[1,8]{1,0:T(1,128)}, u32[]{:S(2)}) copy-start(s32[1,8]{1,0:T(1,128)} %param.16) | copy-start | bytes 100
  5.1 7.7 %copy-start.5 = (s32[86]{0:T(128)S(1)}, s32[86]{0:T(128)}, u32[]{:S(2)}) copy-start(s32[86]{0:T(128)} %get-tuple-element.33.route_ref) | copy-start | bytes 1036
  5.1 8.3 %copy-start.3 = (bf16[32,256]{1,0:T(8,128)(2,1)S(1)}, bf16[32,256]{1,0:T(8,128)(2,1)}, u32[]{:S(2)}) copy-start(bf16[32,256]{1,0:T(8,128)(2,1)} %param.15) | copy-start | bytes 49156
  5.1 8.3 %copy-start.4 = (bf16[32,256]{1,0:T(8,128)(2,1)S(1)}, bf16[32,256]{1,0:T(8,128)(2,1)}, u32[]{:S(2)}) copy-start(bf16[32,256]{1,0:T(8,128)(2,1)} %param.14) | copy-start | bytes 49156
  5.2 57.1 %all-to-all-start.1 = ((bf16[32,64,1024]{2,1,0:T(8,128)(2,1)}), bf16[32,64,1024]{2,1,0:T(8,128)(2,1)}, u32[]{:S(2)}, u32[]{:S(2)}) async-start(bf16[32,64,1024]{2,1,0:T(8,128)(2,1)} %get-tuple-element.34), calls=%async_computation.1 | async-start | bytes 8388608 | tf_op jit(solution)/shard_map/all_to_all | solution.py:567
  63.1 13.3 %collective-permute-start = (bf16[12,64,1024]{2,1,0:T(8,128)(2,1)}, bf16[12,64,1024]{2,1,0:T(8,128)(2,1)}, u32[]{:S(2)}, u32[]{:S(2)}) collective-permute-start(bf16[12,64,1024]{2,1,0:T(8,128)(2,1)} %get-tuple-element.37), channel_id=1, source_target_pairs={{0,4},{1,5},{2,6},{3,7},{4,0},{5,1},{6,2},{7,3},{8,12},{9,13},{10,... | collective-permute-start | bytes 4718600 | tf_op jit(solution)/shard_map/ppermute | solution.py:590
  64.8 11.2 %collective-permute-start.1 = (bf16[2,64,1024]{2,1,0:T(8,128)(2,1)}, bf16[2,64,1024]{2,1,0:T(8,128)(2,1)S(1)}, u32[]{:S(2)}, u32[]{:S(2)}) collective-permute-start(bf16[2,64,1024]{2,1,0:T(8,128)(2,1)} %get-tuple-element.38), channel_id=1, source_target_pairs={{0,1},{1,0},{2,3},{3,2},{4,5},{5,4},{6,7},{7,6},{8,9},{9,8},{10,11... | collective-permute-start | bytes 786440 | tf_op jit(solution)/shard_map/ppermute | solution.py:590
  64.8 11.2 %collective-permute-start.2 = (bf16[2,64,1024]{2,1,0:T(8,128)(2,1)}, bf16[2,64,1024]{2,1,0:T(8,128)(2,1)}, u32[]{:S(2)}, u32[]{:S(2)}) collective-permute-start(bf16[2,64,1024]{2,1,0:T(8,128)(2,1)} %get-tuple-element.39), channel_id=1, source_target_pairs={{0,3},{1,2},{2,1},{3,0},{4,7},{5,6},{6,5},{7,4},{8,11},{9,10},{10,... | collective-permute-start | bytes 786440 | tf_op jit(solution)/shard_map/ppermute | solution.py:590
  66.7 9.3 %collective-permute-start.3 = (bf16[2,64,1024]{2,1,0:T(8,128)(2,1)}, bf16[2,64,1024]{2,1,0:T(8,128)(2,1)}, u32[]{:S(2)}, u32[]{:S(2)}) collective-permute-start(bf16[2,64,1024]{2,1,0:T(8,128)(2,1)} %get-tuple-element.40), channel_id=1, source_target_pairs={{0,8},{1,9},{2,10},{3,11},{4,12},{5,13},{6,14},{7,15},{8,0},{9,1},... | collective-permute-start | bytes 786440 | tf_op jit(solution)/shard_map/ppermute | solution.py:590
  66.7 2.0 %copy-start = (s32[217]{0:T(256)S(1)}, s32[217]{0:T(256)}, u32[]{:S(2)}) copy-start(s32[217]{0:T(256)} %plan.1.table_ref) | copy-start | bytes 2608
  66.7 9.8 %collective-permute-start.4 = (bf16[2,64,1024]{2,1,0:T(8,128)(2,1)}, bf16[2,64,1024]{2,1,0:T(8,128)(2,1)}, u32[]{:S(2)}, u32[]{:S(2)}) collective-permute-start(bf16[2,64,1024]{2,1,0:T(8,128)(2,1)} %get-tuple-element.41), channel_id=1, source_target_pairs={{0,24},{1,25},{2,26},{3,27},{4,28},{5,29},{6,30},{7,31},{8,16},{9,... | collective-permute-start | bytes 786440 | tf_op jit(solution)/shard_map/ppermute | solution.py:590
  68.7 7.8 %copy-start.1 = (bf16[32,64,1024]{2,1,0:T(8,128)(2,1)S(1)}, bf16[32,64,1024]{2,1,0:T(8,128)(2,1)}, u32[]{:S(2)}) copy-start(bf16[32,64,1024]{2,1,0:T(8,128)(2,1)} %get-tuple-element.52.refs_5_) | copy-start | bytes 12582916
